TPU v7x, 32 devices: a whole 2x2x4 slice. The times are simulated.
32 devices in a mesh: rows: 8 (over y, x, core), blk: 4 (over z).
Axes of the slice: x: 2, y: 2, z: 4, core: 2. Of those that a mesh axis runs over, the one named last changes fastest.
Arguments:
- vectors: float32 [6144, 128], P('blk'), may hold values from -6 to 6
- left_intersection: float32 [256, 128, 128], P(('rows', 'blk')), may hold values from -0.5 to 0.5
- right_intersection: float32 [48, 128, 128], P('blk'), may hold values from -0.5 to 0.5
- tiles: float32 [512, 128, 128], P('rows'), may hold values from -0.09375 to 0.09375
- pair_cols: int32 [256, 32], P(('rows', 'blk')), may hold values from 0 to 47, all different within a row
- pair_owner: int32 [256, 32], P(('rows', 'blk')), may hold values from 0 to 7, as said below
- pair_slot: int32 [256, 32], P(('rows', 'blk')), may hold values from 0 to 63
- pair_counts: int32 [256], P(('rows', 'blk')), may hold values from 1 to 32, as said below
Outputs:
- product: float32 [32768, 128], P(('rows', 'blk'))
Inputs may be any that keep to these rules, and one draw needn't show every extreme that they name: `pair_owner`: among the 256 entries of each aligned block of 8 row blocks, every rows index appears exactly 32 times. `pair_cols`: the column blocks listed for one row block are distinct. `pair_counts`: some row block has all 32 entries live.
All inputs are finite; a program needn't handle non-finite values.
Results may differ from a plain program's by a relative error of at most 0.0003.
Values sent between devices are 32-bit elements; how exact they have to be, the bound alone decides.
No kernel may reach another device: no remote copies, remote signals or barrier semaphores. Data moves between devices by JAX's collectives and lax.ppermute only.
A program may use at most 128 MiB of HBM per device.

v0:
```python
import jax
import jax.numpy as jnp
from jax import lax
from jax.sharding import PartitionSpec as P


def pick_rows(table, row_ids, table_rows):
    onehot = (row_ids[:, None] == jnp.arange(table_rows)[None, :]).astype(jnp.float32)
    flat = table.reshape(table_rows, -1)
    picked = jnp.dot(
        onehot, flat, precision=lax.Precision.HIGHEST, preferred_element_type=jnp.float32
    )
    return picked.reshape((row_ids.shape[0],) + table.shape[1:])


def invert_slots(values, slot_index):
    count = slot_index.shape[0]
    matches = slot_index[None, :] == jnp.arange(count)[:, None]
    return jnp.sum(jnp.where(matches, values[None, :], 0), axis=1)


def per_device(
    vectors,
    left_intersection,
    right_intersection,
    tiles,
    pair_cols,
    pair_owner,
    pair_slot,
    pair_counts,
):
    row_blocks, fine_rows, coarse = left_intersection.shape
    listed = pair_cols.shape[1]
    vec_count = vectors.shape[1]
    owners = lax.axis_size("rows")
    entries = row_blocks * listed
    per_owner = entries // owners
    highest = lax.Precision.HIGHEST
    held_tiles = tiles.shape[0]
    flat_owner = pair_owner.reshape(entries)
    earlier = jnp.arange(entries)[:, None] > jnp.arange(entries)[None, :]
    matches = flat_owner[:, None] == flat_owner[None, :]
    position = jnp.sum(jnp.where(matches & earlier, 1, 0), axis=1).astype(jnp.int32)
    slot_index = flat_owner * per_owner + position
    local_blocks = vectors.reshape(right_intersection.shape[0], fine_rows, vec_count)
    entry_ids = jnp.arange(entries)
    block_ids = entry_ids // listed
    count_each = jnp.repeat(pair_counts, listed)
    live_flags = (entry_ids % listed < count_each).astype(jnp.int32)
    block_range = jnp.arange(row_blocks)
    slot_req = invert_slots(pair_slot.reshape(entries), slot_index)
    col_req = invert_slots(pair_cols.reshape(entries), slot_index)
    block_req = invert_slots(block_ids, slot_index)
    live_req = invert_slots(live_flags, slot_index)
    stacked = jnp.stack([slot_req, col_req, block_req, live_req]).reshape(4, owners, per_owner)
    received = lax.all_to_all(stacked, "rows", split_axis=1, concat_axis=1, tiled=True)
    local_proj = jnp.einsum("csu,csv->cuv", right_intersection, local_blocks, precision=highest)
    proj_all = lax.all_gather(local_proj, "blk", axis=0, tiled=True)
    col_total = proj_all.shape[0]

    def per_source(packed):
        slots_here, cols_here, blocks_here, live_here = packed
        chosen = pick_rows(tiles, slots_here, held_tiles)
        picked = pick_rows(proj_all, cols_here, col_total)
        applied = jnp.einsum("ptu,puv->ptv", chosen, picked, precision=highest)
        weights = (
            (blocks_here[None, :] == block_range[:, None]) & (live_here[None, :] > 0)
        ).astype(jnp.float32)
        return jnp.einsum("rp,ptv->rtv", weights, applied, precision=highest)

    partial_sums = lax.map(per_source, (received[0], received[1], received[2], received[3]))
    returned = lax.all_to_all(partial_sums, "rows", split_axis=0, concat_axis=0, tiled=True)
    summed = jnp.sum(returned, axis=0)
    result = jnp.einsum("bft,btv->bfv", left_intersection, summed, precision=highest)
    return result.reshape(row_blocks * fine_rows, vec_count)


def solution(mesh):
    return jax.shard_map(
        per_device,
        mesh=mesh,
        in_specs=(
            P("blk", None),
            P(("rows", "blk"), None, None),
            P("blk", None, None),
            P("rows", None, None),
            P(("rows", "blk"), None),
            P(("rows", "blk"), None),
            P(("rows", "blk"), None),
            P(("rows", "blk")),
        ),
        out_specs=P(("rows", "blk"), None),
        check_vma=False,
    )
```

profile of v0, /device:TPU:0, one launch (start us, length us, event | category | flops | bytes accessed | tf_op | source)
XLA Modules:
  0.0 277.5 jit_solution(6628994686971753800)
XLA Ops:
  6.5 0.0 copy-start
  6.5 0.0 all-gather.2.cloned.1.call-start
  6.6 1.1 copy-done
  7.7 3.4 %fusion.40 = f32[12,128,128]{2,1,0:T(8,128)} fusion(f32[12,128,128]{2,1,0:T(8,128)} %param.12, f32[12,128,128]{2,1,0:T(8,128)S(1)} %bitcast.91), kind=kOutput, calls=%fused_computation.57 | convolution fusion | flops 301989888 | bytes 2359296 | tf_op jit(solution)/shard_map/csu,csv->cuv/dot_general | solution.py:57
  11.1 0.0 all-gather.2.cloned.1.call-update
  11.1 0.0 copy-done.3
  11.1 0.1 reshape.76
  11.2 0.0 copy-done.6
  11.2 0.1 broadcast_in_dim.77
  11.3 0.1 reshape.77
  11.4 0.0 copy-done.4
  11.4 0.1 broadcast_in_dim.72
  11.5 0.0 copy-done.5
  11.5 0.1 broadcast_in_dim.74
  11.5 0.2 select_reduce_fusion.4
  11.7 0.2 select_reduce_fusion.3
  12.0 0.1 stack.15
  12.1 0.1 stack.16
  12.1 0.1 stack.17
  12.2 0.1 stack.18
  12.3 0.7 reshape.85
  13.0 5.2 %all-to-all-start = ((s32[8,1,128]{2,1,0:T(1,128)}), s32[8,1,128]{2,1,0:T(1,128)S(1)}, u32[]{:S(2)}, u32[]{:S(2)}) async-start(s32[8,1,128]{2,1,0:T(1,128)} %reshape.85), calls=%async_computation | async-start | bytes 8192 | tf_op jit(solution)/shard_map/all_to_all | solution.py:56
  18.2 4.6 %all-to-all-done = s32[8,1,128]{2,1,0:T(1,128)S(1)} async-done(((s32[8,1,128]{2,1,0:T(1,128)}), s32[8,1,128]{2,1,0:T(1,128)S(1)}, u32[]{:S(2)}, u32[]{:S(2)}) %all-to-all-start) | async-done | bytes 4128 | tf_op jit(solution)/shard_map/all_to_all | solution.py:56
  22.8 0.5 broadcast.64
  23.3 0.7 reduce
  24.0 0.1 reshape.86
  24.1 53.3 %all-gather.2.cloned.1.call-done = f32[48,128,128]{2,1,0:T(8,128)} async-done(((f32[12,128,128]{2,1,0:T(8,128)}), f32[48,128,128]{2,1,0:T(8,128)}) %all-gather.2.cloned.1.call-update) | async-done | bytes 3145744 | tf_op jit(solution)/shard_map/all_gather | solution.py:58
  77.5 135.7 %while.11 = (s32[]{:T(128)}, f32[8,8,128,128]{3,1,2,0:T(8,128)}, s32[8,32]{1,0:T(8,128)S(1)}, s32[8,32]{1,0:T(8,128)S(1)}, s32[8,32]{1,0:T(8,128)S(1)}, /*index=...) while((s32[]{:T(128)}, f32[8,8,128,128]{3,1,2,0:T(8,128)}, ...), condition=%wide.region_6.7_spmd.clone, body=%wide.region_5.6_spmd.clone.sunk | while | flops 1560285184 | bytes 33032132 | solution.py:71
  77.5 6.2 %fusion.69 = f32[32,128,128]{2,0,1:T(8,128)S(1)} fusion(s32[32]{0:T(128)S(1)} %get-tuple-element.150, f32[8,8,128,128]{3,2,1,0:T(8,128)} %bitcast.92), kind=kOutput, calls=%fused_computation.2.clone.1 | convolution fusion | flops 402655232 | bytes 6291584 | tf_op jit(solution)/shard_map/while/body/eval_jaxpr/dot_general | solution.py:10
  83.7 3.3 %fusion.67 = f32[32,128,128]{2,0,1:T(8,128)S(1)} fusion(s32[32]{0:T(128)S(1)} %fusion.66, f32[6,8,128,128]{3,2,1,0:T(8,128)S(1)} %bitcast.93), kind=kOutput, calls=%fused_computation.6.clone.1 | convolution fusion | flops 301991424 | bytes 5243008 | tf_op jit(solution)/shard_map/while/body/eval_jaxpr/dot_general | solution.py:10
  87.0 4.6 %fusion.70 = f32[32,128,128]{2,1,0:T(8,128)S(1)} fusion(f32[32,128,128]{2,0,1:T(8,128)S(1)} %fusion.67, f32[32,128,128]{2,0,1:T(8,128)S(1)} %fusion.69), kind=kOutput, calls=%fused_computation.11.clone.1 | convolution fusion | flops 805306368 | bytes 6291456 | tf_op jit(solution)/shard_map/while/body/eval_jaxpr/ptu,puv->ptv/dot_general | solution.py:65
  91.6 2.8 fusion.71
  94.4 6.2 %fusion.69 = f32[32,128,128]{2,0,1:T(8,128)S(1)} fusion(s32[32]{0:T(128)S(1)} %get-tuple-element.150, f32[8,8,128,128]{3,2,1,0:T(8,128)} %bitcast.92), kind=kOutput, calls=%fused_computation.2.clone.1 | convolution fusion | flops 402655232 | bytes 6291584 | tf_op jit(solution)/shard_map/while/body/eval_jaxpr/dot_general | solution.py:10
  100.6 3.3 %fusion.67 = f32[32,128,128]{2,0,1:T(8,128)S(1)} fusion(s32[32]{0:T(128)S(1)} %fusion.66, f32[6,8,128,128]{3,2,1,0:T(8,128)S(1)} %bitcast.93), kind=kOutput, calls=%fused_computation.6.clone.1 | convolution fusion | flops 301991424 | bytes 5243008 | tf_op jit(solution)/shard_map/while/body/eval_jaxpr/dot_general | solution.py:10
  104.0 4.6 %fusion.70 = f32[32,128,128]{2,1,0:T(8,128)S(1)} fusion(f32[32,128,128]{2,0,1:T(8,128)S(1)} %fusion.67, f32[32,128,128]{2,0,1:T(8,128)S(1)} %fusion.69), kind=kOutput, calls=%fused_computation.11.clone.1 | convolution fusion | flops 805306368 | bytes 6291456 | tf_op jit(solution)/shard_map/while/body/eval_jaxpr/ptu,puv->ptv/dot_general | solution.py:65
  108.6 2.8 %fusion.71 = f32[8,8,128,128]{3,1,2,0:T(8,128)} fusion(f32[8,8,128,128]{3,1,2,0:T(8,128)} %get-tuple-element.162, s32[]{:T(128)} %get-tuple-element.161, f32[32,128,128]{2,1,0:T(8,128)S(1)} %fusion.70, s32[32]{0:T(128)S(1)} %get-tuple-element.151, pred[32]{0:T(512)(128)(4,1)S(1)} %compare_bitcast_fusion.2), kind=kOutput, calls=%fused_computation.15.clone.1 | convolution fusion | flops 50332160 | bytes 2622112 | tf_op jit(solution)/shard_map/while/body/eval_jaxpr/rp,ptv->rtv/dot_general | solution.py:69
  111.4 6.2 %fusion.69 = f32[32,128,128]{2,0,1:T(8,128)S(1)} fusion(s32[32]{0:T(128)S(1)} %get-tuple-element.150, f32[8,8,128,128]{3,2,1,0:T(8,128)} %bitcast.92), kind=kOutput, calls=%fused_computation.2.clone.1 | convolution fusion | flops 402655232 | bytes 6291584 | tf_op jit(solution)/shard_map/while/body/eval_jaxpr/dot_general | solution.py:10
  117.6 3.3 %fusion.67 = f32[32,128,128]{2,0,1:T(8,128)S(1)} fusion(s32[32]{0:T(128)S(1)} %fusion.66, f32[6,8,128,128]{3,2,1,0:T(8,128)S(1)} %bitcast.93), kind=kOutput, calls=%fused_computation.6.clone.1 | convolution fusion | flops 301991424 | bytes 5243008 | tf_op jit(solution)/shard_map/while/body/eval_jaxpr/dot_general | solution.py:10
  120.9 4.6 %fusion.70 = f32[32,128,128]{2,1,0:T(8,128)S(1)} fusion(f32[32,128,128]{2,0,1:T(8,128)S(1)} %fusion.67, f32[32,128,128]{2,0,1:T(8,128)S(1)} %fusion.69), kind=kOutput, calls=%fused_computation.11.clone.1 | convolution fusion | flops 805306368 | bytes 6291456 | tf_op jit(solution)/shard_map/while/body/eval_jaxpr/ptu,puv->ptv/dot_general | solution.py:65
  125.5 2.8 %fusion.71 = f32[8,8,128,128]{3,1,2,0:T(8,128)} fusion(f32[8,8,128,128]{3,1,2,0:T(8,128)} %get-tuple-element.162, s32[]{:T(128)} %get-tuple-element.161, f32[32,128,128]{2,1,0:T(8,128)S(1)} %fusion.70, s32[32]{0:T(128)S(1)} %get-tuple-element.151, pred[32]{0:T(512)(128)(4,1)S(1)} %compare_bitcast_fusion.2), kind=kOutput, calls=%fused_computation.15.clone.1 | convolution fusion | flops 50332160 | bytes 2622112 | tf_op jit(solution)/shard_map/while/body/eval_jaxpr/rp,ptv->rtv/dot_general | solution.py:69
  128.3 6.2 %fusion.69 = f32[32,128,128]{2,0,1:T(8,128)S(1)} fusion(s32[32]{0:T(128)S(1)} %get-tuple-element.150, f32[8,8,128,128]{3,2,1,0:T(8,128)} %bitcast.92), kind=kOutput, calls=%fused_computation.2.clone.1 | convolution fusion | flops 402655232 | bytes 6291584 | tf_op jit(solution)/shard_map/while/body/eval_jaxpr/dot_general | solution.py:10
  134.6 3.3 %fusion.67 = f32[32,128,128]{2,0,1:T(8,128)S(1)} fusion(s32[32]{0:T(128)S(1)} %fusion.66, f32[6,8,128,128]{3,2,1,0:T(8,128)S(1)} %bitcast.93), kind=kOutput, calls=%fused_computation.6.clone.1 | convolution fusion | flops 301991424 | bytes 5243008 | tf_op jit(solution)/shard_map/while/body/eval_jaxpr/dot_general | solution.py:10
  137.9 4.6 %fusion.70 = f32[32,128,128]{2,1,0:T(8,128)S(1)} fusion(f32[32,128,128]{2,0,1:T(8,128)S(1)} %fusion.67, f32[32,128,128]{2,0,1:T(8,128)S(1)} %fusion.69), kind=kOutput, calls=%fused_computation.11.clone.1 | convolution fusion | flops 805306368 | bytes 6291456 | tf_op jit(solution)/shard_map/while/body/eval_jaxpr/ptu,puv->ptv/dot_general | solution.py:65
  142.5 2.8 %fusion.71 = f32[8,8,128,128]{3,1,2,0:T(8,128)} fusion(f32[8,8,128,128]{3,1,2,0:T(8,128)} %get-tuple-element.162, s32[]{:T(128)} %get-tuple-element.161, f32[32,128,128]{2,1,0:T(8,128)S(1)} %fusion.70, s32[32]{0:T(128)S(1)} %get-tuple-element.151, pred[32]{0:T(512)(128)(4,1)S(1)} %compare_bitcast_fusion.2), kind=kOutput, calls=%fused_computation.15.clone.1 | convolution fusion | flops 50332160 | bytes 2622112 | tf_op jit(solution)/shard_map/while/body/eval_jaxpr/rp,ptv->rtv/dot_general | solution.py:69
  145.3 6.2 %fusion.69 = f32[32,128,128]{2,0,1:T(8,128)S(1)} fusion(s32[32]{0:T(128)S(1)} %get-tuple-element.150, f32[8,8,128,128]{3,2,1,0:T(8,128)} %bitcast.92), kind=kOutput, calls=%fused_computation.2.clone.1 | convolution fusion | flops 402655232 | bytes 6291584 | tf_op jit(solution)/shard_map/while/body/eval_jaxpr/dot_general | solution.py:10
  151.5 3.3 %fusion.67 = f32[32,128,128]{2,0,1:T(8,128)S(1)} fusion(s32[32]{0:T(128)S(1)} %fusion.66, f32[6,8,128,128]{3,2,1,0:T(8,128)S(1)} %bitcast.93), kind=kOutput, calls=%fused_computation.6.clone.1 | convolution fusion | flops 301991424 | bytes 5243008 | tf_op jit(solution)/shard_map/while/body/eval_jaxpr/dot_general | solution.py:10
  154.9 4.6 %fusion.70 = f32[32,128,128]{2,1,0:T(8,128)S(1)} fusion(f32[32,128,128]{2,0,1:T(8,128)S(1)} %fusion.67, f32[32,128,128]{2,0,1:T(8,128)S(1)} %fusion.69), kind=kOutput, calls=%fused_computation.11.clone.1 | convolution fusion | flops 805306368 | bytes 6291456 | tf_op jit(solution)/shard_map/while/body/eval_jaxpr/ptu,puv->ptv/dot_general | solution.py:65
  159.5 2.8 fusion.71
  162.2 6.2 %fusion.69 = f32[32,128,128]{2,0,1:T(8,128)S(1)} fusion(s32[32]{0:T(128)S(1)} %get-tuple-element.150, f32[8,8,128,128]{3,2,1,0:T(8,128)} %bitcast.92), kind=kOutput, calls=%fused_computation.2.clone.1 | convolution fusion | flops 402655232 | bytes 6291584 | tf_op jit(solution)/shard_map/while/body/eval_jaxpr/dot_general | solution.py:10
  168.5 3.3 %fusion.67 = f32[32,128,128]{2,0,1:T(8,128)S(1)} fusion(s32[32]{0:T(128)S(1)} %fusion.66, f32[6,8,128,128]{3,2,1,0:T(8,128)S(1)} %bitcast.93), kind=kOutput, calls=%fused_computation.6.clone.1 | convolution fusion | flops 301991424 | bytes 5243008 | tf_op jit(solution)/shard_map/while/body/eval_jaxpr/dot_general | solution.py:10
  171.8 4.6 %fusion.70 = f32[32,128,128]{2,1,0:T(8,128)S(1)} fusion(f32[32,128,128]{2,0,1:T(8,128)S(1)} %fusion.67, f32[32,128,128]{2,0,1:T(8,128)S(1)} %fusion.69), kind=kOutput, calls=%fused_computation.11.clone.1 | convolution fusion | flops 805306368 | bytes 6291456 | tf_op jit(solution)/shard_map/while/body/eval_jaxpr/ptu,puv->ptv/dot_general | solution.py:65
  176.4 2.8 %fusion.71 = f32[8,8,128,128]{3,1,2,0:T(8,128)} fusion(f32[8,8,128,128]{3,1,2,0:T(8,128)} %get-tuple-element.162, s32[]{:T(128)} %get-tuple-element.161, f32[32,128,128]{2,1,0:T(8,128)S(1)} %fusion.70, s32[32]{0:T(128)S(1)} %get-tuple-element.151, pred[32]{0:T(512)(128)(4,1)S(1)} %compare_bitcast_fusion.2), kind=kOutput, calls=%fused_computation.15.clone.1 | convolution fusion | flops 50332160 | bytes 2622112 | tf_op jit(solution)/shard_map/while/body/eval_jaxpr/rp,ptv->rtv/dot_general | solution.py:69
  179.2 6.2 %fusion.69 = f32[32,128,128]{2,0,1:T(8,128)S(1)} fusion(s32[32]{0:T(128)S(1)} %get-tuple-element.150, f32[8,8,128,128]{3,2,1,0:T(8,128)} %bitcast.92), kind=kOutput, calls=%fused_computation.2.clone.1 | convolution fusion | flops 402655232 | bytes 6291584 | tf_op jit(solution)/shard_map/while/body/eval_jaxpr/dot_general | solution.py:10
  185.4 0.0 copy-done.1
  185.5 3.3 %fusion.67 = f32[32,128,128]{2,0,1:T(8,128)S(1)} fusion(s32[32]{0:T(128)S(1)} %fusion.66, f32[6,8,128,128]{3,2,1,0:T(8,128)S(1)} %bitcast.93), kind=kOutput, calls=%fused_computation.6.clone.1 | convolution fusion | flops 301991424 | bytes 5243008 | tf_op jit(solution)/shard_map/while/body/eval_jaxpr/dot_general | solution.py:10
  188.8 4.6 %fusion.70 = f32[32,128,128]{2,1,0:T(8,128)S(1)} fusion(f32[32,128,128]{2,0,1:T(8,128)S(1)} %fusion.67, f32[32,128,128]{2,0,1:T(8,128)S(1)} %fusion.69), kind=kOutput, calls=%fused_computation.11.clone.1 | convolution fusion | flops 805306368 | bytes 6291456 | tf_op jit(solution)/shard_map/while/body/eval_jaxpr/ptu,puv->ptv/dot_general | solution.py:65
  193.4 2.8 fusion.71
  196.1 6.2 %fusion.69 = f32[32,128,128]{2,0,1:T(8,128)S(1)} fusion(s32[32]{0:T(128)S(1)} %get-tuple-element.150, f32[8,8,128,128]{3,2,1,0:T(8,128)} %bitcast.92), kind=kOutput, calls=%fused_computation.2.clone.1 | convolution fusion | flops 402655232 | bytes 6291584 | tf_op jit(solution)/shard_map/while/body/eval_jaxpr/dot_general | solution.py:10
  202.4 3.3 %fusion.67 = f32[32,128,128]{2,0,1:T(8,128)S(1)} fusion(s32[32]{0:T(128)S(1)} %fusion.66, f32[6,8,128,128]{3,2,1,0:T(8,128)S(1)} %bitcast.93), kind=kOutput, calls=%fused_computation.6.clone.1 | convolution fusion | flops 301991424 | bytes 5243008 | tf_op jit(solution)/shard_map/while/body/eval_jaxpr/dot_general | solution.py:10
  205.7 4.6 %fusion.70 = f32[32,128,128]{2,1,0:T(8,128)S(1)} fusion(f32[32,128,128]{2,0,1:T(8,128)S(1)} %fusion.67, f32[32,128,128]{2,0,1:T(8,128)S(1)} %fusion.69), kind=kOutput, calls=%fused_computation.11.clone.1 | convolution fusion | flops 805306368 | bytes 6291456 | tf_op jit(solution)/shard_map/while/body/eval_jaxpr/ptu,puv->ptv/dot_general | solution.py:65
  210.3 2.8 %fusion.71 = f32[8,8,128,128]{3,1,2,0:T(8,128)} fusion(f32[8,8,128,128]{3,1,2,0:T(8,128)} %get-tuple-element.162, s32[]{:T(128)} %get-tuple-element.161, f32[32,128,128]{2,1,0:T(8,128)S(1)} %fusion.70, s32[32]{0:T(128)S(1)} %get-tuple-element.151, pred[32]{0:T(512)(128)(4,1)S(1)} %compare_bitcast_fusion.2), kind=kOutput, calls=%fused_computation.15.clone.1 | convolution fusion | flops 50332160 | bytes 2622112 | tf_op jit(solution)/shard_map/while/body/eval_jaxpr/rp,ptv->rtv/dot_general | solution.py:69
  213.1 53.5 %all_to_all.10 = f32[8,8,128,128]{3,1,2,0:T(8,128)} all-to-all(f32[8,8,128,128]{3,1,2,0:T(8,128)} %get-tuple-element.52), channel_id=1, replica_groups=mesh['rows'=8,'blk'=4] {'rows'}, dimensions={0} | all-to-all | bytes 8388608 | tf_op jit(solution)/shard_map/all_to_all | solution.py:72
  266.6 2.5 reduce_sum.59
  269.1 1.5 fusion.33
  (50 shorter events, 0.3 us)
Async XLA Ops:
  6.5 1.1 copy-start
  6.5 4.6 %copy-start.3 = (s32[8,32]{1,0:T(8,128)S(1)}, s32[8,32]{1,0:T(8,128)}, u32[]{:S(2)}) copy-start(s32[8,32]{1,0:T(8,128)} %param.15) | copy-start | bytes 3076
  6.5 4.7 %copy-start.6 = (s32[8]{0:T(128)S(1)}, s32[8]{0:T(128)}, u32[]{:S(2)}) copy-start(s32[8]{0:T(128)} %param.17) | copy-start | bytes 100
  6.5 4.8 %copy-start.4 = (s32[8,32]{1,0:T(8,128)S(1)}, s32[8,32]{1,0:T(8,128)}, u32[]{:S(2)}) copy-start(s32[8,32]{1,0:T(8,128)} %param.16) | copy-start | bytes 3076
  6.5 4.9 %copy-start.5 = (s32[8,32]{1,0:T(8,128)S(1)}, s32[8,32]{1,0:T(8,128)}, u32[]{:S(2)}) copy-start(s32[8,32]{1,0:T(8,128)} %param.14) | copy-start | bytes 3076
  6.5 70.9 %all-gather.2.cloned.1.call-start = ((), (), s32[]{:S(2)}) async-start(), calls=%async_computation.2 | async-start | bytes 3932160 | tf_op jit(solution)/shard_map/all_gather | solution.py:58
  13.0 9.8 %all-to-all-start = ((s32[8,1,128]{2,1,0:T(1,128)}), s32[8,1,128]{2,1,0:T(1,128)S(1)}, u32[]{:S(2)}, u32[]{:S(2)}) async-start(s32[8,1,128]{2,1,0:T(1,128)} %reshape.85), calls=%async_computation | async-start | bytes 8192 | tf_op jit(solution)/shard_map/all_to_all | solution.py:56
  77.5 6.2 %copy-start.1 = (f32[48,128,128]{2,1,0:T(8,128)S(1)}, f32[48,128,128]{2,1,0:T(8,128)}, u32[]{:S(2)}) copy-start(f32[48,128,128]{2,1,0:T(8,128)} %get-tuple-element.177) | copy-start | bytes 9437188 | tf_op jit(solution)/shard_map/while
  94.4 6.2 %copy-start.1 = (f32[48,128,128]{2,1,0:T(8,128)S(1)}, f32[48,128,128]{2,1,0:T(8,128)}, u32[]{:S(2)}) copy-start(f32[48,128,128]{2,1,0:T(8,128)} %get-tuple-element.177) | copy-start | bytes 9437188 | tf_op jit(solution)/shard_map/while
  111.4 6.2 %copy-start.1 = (f32[48,128,128]{2,1,0:T(8,128)S(1)}, f32[48,128,128]{2,1,0:T(8,128)}, u32[]{:S(2)}) copy-start(f32[48,128,128]{2,1,0:T(8,128)} %get-tuple-element.177) | copy-start | bytes 9437188 | tf_op jit(solution)/shard_map/while
  128.3 6.2 %copy-start.1 = (f32[48,128,128]{2,1,0:T(8,128)S(1)}, f32[48,128,128]{2,1,0:T(8,128)}, u32[]{:S(2)}) copy-start(f32[48,128,128]{2,1,0:T(8,128)} %get-tuple-element.177) | copy-start | bytes 9437188 | tf_op jit(solution)/shard_map/while
  145.3 6.2 %copy-start.1 = (f32[48,128,128]{2,1,0:T(8,128)S(1)}, f32[48,128,128]{2,1,0:T(8,128)}, u32[]{:S(2)}) copy-start(f32[48,128,128]{2,1,0:T(8,128)} %get-tuple-element.177) | copy-start | bytes 9437188 | tf_op jit(solution)/shard_map/while
  162.2 6.2 %copy-start.1 = (f32[48,128,128]{2,1,0:T(8,128)S(1)}, f32[48,128,128]{2,1,0:T(8,128)}, u32[]{:S(2)}) copy-start(f32[48,128,128]{2,1,0:T(8,128)} %get-tuple-element.177) | copy-start | bytes 9437188 | tf_op jit(solution)/shard_map/while
  179.2 6.2 %copy-start.1 = (f32[48,128,128]{2,1,0:T(8,128)S(1)}, f32[48,128,128]{2,1,0:T(8,128)}, u32[]{:S(2)}) copy-start(f32[48,128,128]{2,1,0:T(8,128)} %get-tuple-element.177) | copy-start | bytes 9437188 | tf_op jit(solution)/shard_map/while
  196.1 6.2 %copy-start.1 = (f32[48,128,128]{2,1,0:T(8,128)S(1)}, f32[48,128,128]{2,1,0:T(8,128)}, u32[]{:S(2)}) copy-start(f32[48,128,128]{2,1,0:T(8,128)} %get-tuple-element.177) | copy-start | bytes 9437188 | tf_op jit(solution)/shard_map/while
  266.6 2.5 copy-start.2
Sparse Core Ops, SparseCore 0:
  11.2 66.1 all-gather.1
where the time goes:
time: 278 us; the launch traced here: 277 us
  matrix products  140 us (50%)
  waiting for transfers between devices  58 us (21%)
  blocking collectives  53.5 us (19%)
  between operations  13.5 us (5%)
  starting transfers between devices  5.24 us (2%)
  other arithmetic  3.71 us (1%)
  local copies, waits for them, and re-layouts  3.25 us (1%)
    dot_general x16, matrix products, pick_rows(): jnp.dot(onehot, flat, precision=lax.Precision.HIGHEST, preferred_element_...  76.3 us
    all_to_all x1, blocking collectives, per_device(): lax.all_to_all(partial_sums, 'rows', split_axis=0, concat_axis=0, tiled=T...  53.5 us
    all_gather x1, waiting for transfers between devices, per_device(): proj_all = lax.all_gather(local_proj, 'blk', axis=0, tiled=True)  53.3 us
    dot_general x8, matrix products, per_source(): applied = jnp.einsum('ptu,puv->ptv', chosen, picked, precision=highest)  36.6 us
    dot_general x8, matrix products, per_source(): return jnp.einsum('rp,ptv->rtv', weights, applied, precision=highest)  22.2 us
  transfers between devices with their start and end apart: 2, of which 2 were waited for; matrix products, arithmetic and copies ran while one was open for 1% of the time, Pallas kernels for 0%

commit v1 on v0

--- a/solution.py
+++ b/solution.py
@@ -2,6 +2,18 @@
 import jax.numpy as jnp
 from jax import lax
 from jax.sharding import PartitionSpec as P
+
+
+def widths_report(x_part, dim_i, mat):
+    d_next, work_now = (x_part.shape[:dim_i], x_part.shape[dim_i + 1 :])
+    mat_out = x_part.reshape(*d_next, mat, -1, *work_now)
+    return jnp.moveaxis(mat_out, dim_i, 0)
+
+
+def _solve_region(local, pos_dim):
+    local = jnp.moveaxis(local, 0, pos_dim)
+    w2 = local.shape
+    return local.reshape(*w2[:pos_dim], w2[pos_dim] * w2[pos_dim + 1], *w2[pos_dim + 2 :])
 
 
 def pick_rows(table, row_ids, table_rows):
@@ -53,7 +65,20 @@
     block_req = invert_slots(block_ids, slot_index)
     live_req = invert_slots(live_flags, slot_index)
     stacked = jnp.stack([slot_req, col_req, block_req, live_req]).reshape(4, owners, per_owner)
-    received = lax.all_to_all(stacked, "rows", split_axis=1, concat_axis=1, tiled=True)
+    local_now = lax.axis_size("rows")
+    ready = lax.axis_index("rows")
+    n_now, val2 = (local_now, ready)
+    top = widths_report(stacked, 1, n_now)
+    m = 1
+    pages = [top[val2]]
+    while m < n_now:
+        arr_now = top[val2 ^ m]
+        q_next = lax.ppermute(arr_now, axis_name="rows", perm=[(jj, jj ^ m) for jj in range(n_now)])
+        pages.append(q_next)
+        m += 1
+    oldest = jnp.stack(pages)
+    top = oldest[val2 ^ jnp.arange(n_now)]
+    received = _solve_region(top, 1)
     local_proj = jnp.einsum("csu,csv->cuv", right_intersection, local_blocks, precision=highest)
     proj_all = lax.all_gather(local_proj, "blk", axis=0, tiled=True)
     col_total = proj_all.shape[0]

time: 278 us -> 278 us (level)
    ppermute x0 -> x7, starting transfers between devices: none -> 7.75 us  [per_device(): lax.ppermute(arr_now, axis_name='rows', perm=[(jj, jj ^ m) for jj in rang...]
    all_to_all x1 -> x0, starting transfers between devices: 5.2 us -> none  [per_device(): lax.all_to_all(stacked, 'rows', split_axis=1, concat_axis=1, tiled=True)]
    all_to_all x1 -> x0, waiting for transfers between devices: 4.61 us -> none  [per_device(): lax.all_to_all(stacked, 'rows', split_axis=1, concat_axis=1, tiled=True)]
    ppermute x0 -> x7, waiting for transfers between devices: none -> 3.74 us  [per_device(): lax.ppermute(arr_now, axis_name='rows', perm=[(jj, jj ^ m) for jj in rang...]
  transfers between devices with their start and end apart: 2 -> 8, of which waited for: 2 -> 4; matrix products, arithmetic and copies ran while one was open for 1% -> 1% of each run, Pallas kernels for 0% -> 0%
where the time goes in v1:
time: 278 us; the launch traced here: 277 us
  matrix products  140 us (50%)
  waiting for transfers between devices  56.6 us (20%)
  blocking collectives  53.5 us (19%)
  between operations  13.5 us (5%)
  starting transfers between devices  7.79 us (3%)
  other arithmetic  3.07 us (1%)
    dot_general x16, matrix products, pick_rows(): jnp.dot(onehot, flat, precision=lax.Precision.HIGHEST, preferred_element_...  76.3 us
    all_to_all x1, blocking collectives, per_device(): lax.all_to_all(partial_sums, 'rows', split_axis=0, concat_axis=0, tiled=T...  53.5 us
    all_gather x1, waiting for transfers between devices, per_device(): proj_all = lax.all_gather(local_proj, 'blk', axis=0, tiled=True)  52.8 us
    dot_general x8, matrix products, per_source(): applied = jnp.einsum('ptu,puv->ptv', chosen, picked, precision=highest)  36.6 us
    dot_general x8, matrix products, per_source(): return jnp.einsum('rp,ptv->rtv', weights, applied, precision=highest)  22.1 us
    ppermute x7, starting transfers between devices, per_device(): lax.ppermute(arr_now, axis_name='rows', perm=[(jj, jj ^ m) for jj in rang...  7.75 us
  transfers between devices with their start and end apart: 8, of which 4 were waited for; matrix products, arithmetic and copies ran while one was open for 1% of the time, Pallas kernels for 0%

profile of v1, /device:TPU:0, one launch (start us, length us, event | category | flops | bytes accessed | tf_op | source)
XLA Modules:
  0.0 277.4 jit_solution(7954333062043693140)
XLA Ops:
  6.5 0.0 all-gather.2.cloned.1.call-start
  6.6 1.1 copy-done
  7.7 3.5 %fusion.40 = f32[12,128,128]{2,1,0:T(8,128)} fusion(f32[12,128,128]{2,1,0:T(8,128)} %param.12, f32[12,128,128]{2,1,0:T(8,128)S(1)} %bitcast.124), kind=kOutput, calls=%fused_computation.75 | convolution fusion | flops 301989888 | bytes 2359296 | tf_op jit(solution)/shard_map/csu,csv->cuv/dot_general | solution.py:82
  11.1 0.0 all-gather.2.cloned.1.call-update
  11.2 0.1 reshape.115
  11.3 0.1 broadcast_in_dim.78
  11.3 0.1 reshape.116
  11.4 0.1 broadcast_in_dim.73
  11.5 0.1 broadcast_in_dim.75
  11.6 0.2 select_reduce_fusion.4
  11.8 0.2 select_reduce_fusion.3
  12.0 0.1 stack.39
  12.1 0.1 stack.40
  12.2 0.1 stack.41
  12.3 0.1 stack.42
  12.4 0.6 collective-permute-start
  13.0 2.6 collective-permute-start.1
  15.5 0.0 collective-permute-start.2
  15.6 1.8 collective-permute-start.3
  17.4 0.0 collective-permute-done
  17.4 2.7 collective-permute-start.5
  20.1 0.0 collective-permute-done.1
  20.1 0.1 collective-permute-start.6
  20.3 0.1 collective-permute-done.4
  20.4 1.6 collective-permute-done.5
  22.0 2.1 collective-permute-done.6
  24.0 0.6 gather_fusion
  24.6 52.8 %all-gather.2.cloned.1.call-done = f32[48,128,128]{2,1,0:T(8,128)} async-done(((f32[12,128,128]{2,1,0:T(8,128)}), f32[48,128,128]{2,1,0:T(8,128)}) %all-gather.2.cloned.1.call-update) | async-done | bytes 3145744 | tf_op jit(solution)/shard_map/all_gather | solution.py:83
  77.5 135.6 %while.11 = (s32[]{:T(128)}, f32[8,8,128,128]{3,1,2,0:T(8,128)}, s32[8,32]{1,0:T(8,128)S(1)}, s32[8,32]{1,0:T(8,128)S(1)}, s32[8,32]{1,0:T(8,128)S(1)}, /*index=...) while((s32[]{:T(128)}, f32[8,8,128,128]{3,1,2,0:T(8,128)}, ...), condition=%wide.region_6.7_spmd.clone, body=%wide.region_5.6_spmd.clone.sunk | while | flops 1560285184 | bytes 33032132 | solution.py:96
  77.5 6.2 %fusion.69 = f32[32,128,128]{2,0,1:T(8,128)S(1)} fusion(s32[32]{0:T(128)S(1)} %get-tuple-element.157, f32[8,8,128,128]{3,2,1,0:T(8,128)} %bitcast.125), kind=kOutput, calls=%fused_computation.3.clone.1 | convolution fusion | flops 402655232 | bytes 6291584 | tf_op jit(solution)/shard_map/while/body/eval_jaxpr/dot_general | solution.py:22
  83.7 3.3 %fusion.67 = f32[32,128,128]{2,0,1:T(8,128)S(1)} fusion(s32[32]{0:T(128)S(1)} %fusion.66, f32[6,8,128,128]{3,2,1,0:T(8,128)S(1)} %bitcast.126), kind=kOutput, calls=%fused_computation.7.clone.1 | convolution fusion | flops 301991424 | bytes 5243008 | tf_op jit(solution)/shard_map/while/body/eval_jaxpr/dot_general | solution.py:22
  87.1 4.6 %fusion.70 = f32[32,128,128]{2,1,0:T(8,128)S(1)} fusion(f32[32,128,128]{2,0,1:T(8,128)S(1)} %fusion.67, f32[32,128,128]{2,0,1:T(8,128)S(1)} %fusion.69), kind=kOutput, calls=%fused_computation.12.clone.1 | convolution fusion | flops 805306368 | bytes 6291456 | tf_op jit(solution)/shard_map/while/body/eval_jaxpr/ptu,puv->ptv/dot_general | solution.py:90
  91.7 2.8 fusion.71
  94.4 6.2 %fusion.69 = f32[32,128,128]{2,0,1:T(8,128)S(1)} fusion(s32[32]{0:T(128)S(1)} %get-tuple-element.157, f32[8,8,128,128]{3,2,1,0:T(8,128)} %bitcast.125), kind=kOutput, calls=%fused_computation.3.clone.1 | convolution fusion | flops 402655232 | bytes 6291584 | tf_op jit(solution)/shard_map/while/body/eval_jaxpr/dot_general | solution.py:22
  100.7 3.3 %fusion.67 = f32[32,128,128]{2,0,1:T(8,128)S(1)} fusion(s32[32]{0:T(128)S(1)} %fusion.66, f32[6,8,128,128]{3,2,1,0:T(8,128)S(1)} %bitcast.126), kind=kOutput, calls=%fused_computation.7.clone.1 | convolution fusion | flops 301991424 | bytes 5243008 | tf_op jit(solution)/shard_map/while/body/eval_jaxpr/dot_general | solution.py:22
  104.0 4.6 %fusion.70 = f32[32,128,128]{2,1,0:T(8,128)S(1)} fusion(f32[32,128,128]{2,0,1:T(8,128)S(1)} %fusion.67, f32[32,128,128]{2,0,1:T(8,128)S(1)} %fusion.69), kind=kOutput, calls=%fused_computation.12.clone.1 | convolution fusion | flops 805306368 | bytes 6291456 | tf_op jit(solution)/shard_map/while/body/eval_jaxpr/ptu,puv->ptv/dot_general | solution.py:90
  108.6 2.8 fusion.71
  111.4 6.2 %fusion.69 = f32[32,128,128]{2,0,1:T(8,128)S(1)} fusion(s32[32]{0:T(128)S(1)} %get-tuple-element.157, f32[8,8,128,128]{3,2,1,0:T(8,128)} %bitcast.125), kind=kOutput, calls=%fused_computation.3.clone.1 | convolution fusion | flops 402655232 | bytes 6291584 | tf_op jit(solution)/shard_map/while/body/eval_jaxpr/dot_general | solution.py:22
  117.6 3.3 %fusion.67 = f32[32,128,128]{2,0,1:T(8,128)S(1)} fusion(s32[32]{0:T(128)S(1)} %fusion.66, f32[6,8,128,128]{3,2,1,0:T(8,128)S(1)} %bitcast.126), kind=kOutput, calls=%fused_computation.7.clone.1 | convolution fusion | flops 301991424 | bytes 5243008 | tf_op jit(solution)/shard_map/while/body/eval_jaxpr/dot_general | solution.py:22
  120.9 4.6 %fusion.70 = f32[32,128,128]{2,1,0:T(8,128)S(1)} fusion(f32[32,128,128]{2,0,1:T(8,128)S(1)} %fusion.67, f32[32,128,128]{2,0,1:T(8,128)S(1)} %fusion.69), kind=kOutput, calls=%fused_computation.12.clone.1 | convolution fusion | flops 805306368 | bytes 6291456 | tf_op jit(solution)/shard_map/while/body/eval_jaxpr/ptu,puv->ptv/dot_general | solution.py:90
  125.5 2.8 fusion.71
  128.3 6.2 %fusion.69 = f32[32,128,128]{2,0,1:T(8,128)S(1)} fusion(s32[32]{0:T(128)S(1)} %get-tuple-element.157, f32[8,8,128,128]{3,2,1,0:T(8,128)} %bitcast.125), kind=kOutput, calls=%fused_computation.3.clone.1 | convolution fusion | flops 402655232 | bytes 6291584 | tf_op jit(solution)/shard_map/while/body/eval_jaxpr/dot_general | solution.py:22
  134.6 3.3 %fusion.67 = f32[32,128,128]{2,0,1:T(8,128)S(1)} fusion(s32[32]{0:T(128)S(1)} %fusion.66, f32[6,8,128,128]{3,2,1,0:T(8,128)S(1)} %bitcast.126), kind=kOutput, calls=%fused_computation.7.clone.1 | convolution fusion | flops 301991424 | bytes 5243008 | tf_op jit(solution)/shard_map/while/body/eval_jaxpr/dot_general | solution.py:22
  137.9 4.6 %fusion.70 = f32[32,128,128]{2,1,0:T(8,128)S(1)} fusion(f32[32,128,128]{2,0,1:T(8,128)S(1)} %fusion.67, f32[32,128,128]{2,0,1:T(8,128)S(1)} %fusion.69), kind=kOutput, calls=%fused_computation.12.clone.1 | convolution fusion | flops 805306368 | bytes 6291456 | tf_op jit(solution)/shard_map/while/body/eval_jaxpr/ptu,puv->ptv/dot_general | solution.py:90
  142.5 2.8 fusion.71
  145.3 6.2 %fusion.69 = f32[32,128,128]{2,0,1:T(8,128)S(1)} fusion(s32[32]{0:T(128)S(1)} %get-tuple-element.157, f32[8,8,128,128]{3,2,1,0:T(8,128)} %bitcast.125), kind=kOutput, calls=%fused_computation.3.clone.1 | convolution fusion | flops 402655232 | bytes 6291584 | tf_op jit(solution)/shard_map/while/body/eval_jaxpr/dot_general | solution.py:22
  151.5 3.3 %fusion.67 = f32[32,128,128]{2,0,1:T(8,128)S(1)} fusion(s32[32]{0:T(128)S(1)} %fusion.66, f32[6,8,128,128]{3,2,1,0:T(8,128)S(1)} %bitcast.126), kind=kOutput, calls=%fused_computation.7.clone.1 | convolution fusion | flops 301991424 | bytes 5243008 | tf_op jit(solution)/shard_map/while/body/eval_jaxpr/dot_general | solution.py:22
  154.8 4.6 %fusion.70 = f32[32,128,128]{2,1,0:T(8,128)S(1)} fusion(f32[32,128,128]{2,0,1:T(8,128)S(1)} %fusion.67, f32[32,128,128]{2,0,1:T(8,128)S(1)} %fusion.69), kind=kOutput, calls=%fused_computation.12.clone.1 | convolution fusion | flops 805306368 | bytes 6291456 | tf_op jit(solution)/shard_map/while/body/eval_jaxpr/ptu,puv->ptv/dot_general | solution.py:90
  159.4 2.8 fusion.71
  162.2 6.2 %fusion.69 = f32[32,128,128]{2,0,1:T(8,128)S(1)} fusion(s32[32]{0:T(128)S(1)} %get-tuple-element.157, f32[8,8,128,128]{3,2,1,0:T(8,128)} %bitcast.125), kind=kOutput, calls=%fused_computation.3.clone.1 | convolution fusion | flops 402655232 | bytes 6291584 | tf_op jit(solution)/shard_map/while/body/eval_jaxpr/dot_general | solution.py:22
  168.4 3.3 %fusion.67 = f32[32,128,128]{2,0,1:T(8,128)S(1)} fusion(s32[32]{0:T(128)S(1)} %fusion.66, f32[6,8,128,128]{3,2,1,0:T(8,128)S(1)} %bitcast.126), kind=kOutput, calls=%fused_computation.7.clone.1 | convolution fusion | flops 301991424 | bytes 5243008 | tf_op jit(solution)/shard_map/while/body/eval_jaxpr/dot_general | solution.py:22
  171.8 4.6 %fusion.70 = f32[32,128,128]{2,1,0:T(8,128)S(1)} fusion(f32[32,128,128]{2,0,1:T(8,128)S(1)} %fusion.67, f32[32,128,128]{2,0,1:T(8,128)S(1)} %fusion.69), kind=kOutput, calls=%fused_computation.12.clone.1 | convolution fusion | flops 805306368 | bytes 6291456 | tf_op jit(solution)/shard_map/while/body/eval_jaxpr/ptu,puv->ptv/dot_general | solution.py:90
  176.4 2.8 fusion.71
  179.2 6.2 %fusion.69 = f32[32,128,128]{2,0,1:T(8,128)S(1)} fusion(s32[32]{0:T(128)S(1)} %get-tuple-element.157, f32[8,8,128,128]{3,2,1,0:T(8,128)} %bitcast.125), kind=kOutput, calls=%fused_computation.3.clone.1 | convolution fusion | flops 402655232 | bytes 6291584 | tf_op jit(solution)/shard_map/while/body/eval_jaxpr/dot_general | solution.py:22
  185.4 3.3 %fusion.67 = f32[32,128,128]{2,0,1:T(8,128)S(1)} fusion(s32[32]{0:T(128)S(1)} %fusion.66, f32[6,8,128,128]{3,2,1,0:T(8,128)S(1)} %bitcast.126), kind=kOutput, calls=%fused_computation.7.clone.1 | convolution fusion | flops 301991424 | bytes 5243008 | tf_op jit(solution)/shard_map/while/body/eval_jaxpr/dot_general | solution.py:22
  188.7 4.6 %fusion.70 = f32[32,128,128]{2,1,0:T(8,128)S(1)} fusion(f32[32,128,128]{2,0,1:T(8,128)S(1)} %fusion.67, f32[32,128,128]{2,0,1:T(8,128)S(1)} %fusion.69), kind=kOutput, calls=%fused_computation.12.clone.1 | convolution fusion | flops 805306368 | bytes 6291456 | tf_op jit(solution)/shard_map/while/body/eval_jaxpr/ptu,puv->ptv/dot_general | solution.py:90
  193.3 2.8 fusion.71
  196.1 6.2 %fusion.69 = f32[32,128,128]{2,0,1:T(8,128)S(1)} fusion(s32[32]{0:T(128)S(1)} %get-tuple-element.157, f32[8,8,128,128]{3,2,1,0:T(8,128)} %bitcast.125), kind=kOutput, calls=%fused_computation.3.clone.1 | convolution fusion | flops 402655232 | bytes 6291584 | tf_op jit(solution)/shard_map/while/body/eval_jaxpr/dot_general | solution.py:22
  202.3 3.3 %fusion.67 = f32[32,128,128]{2,0,1:T(8,128)S(1)} fusion(s32[32]{0:T(128)S(1)} %fusion.66, f32[6,8,128,128]{3,2,1,0:T(8,128)S(1)} %bitcast.126), kind=kOutput, calls=%fused_computation.7.clone.1 | convolution fusion | flops 301991424 | bytes 5243008 | tf_op jit(solution)/shard_map/while/body/eval_jaxpr/dot_general | solution.py:22
  205.7 4.6 %fusion.70 = f32[32,128,128]{2,1,0:T(8,128)S(1)} fusion(f32[32,128,128]{2,0,1:T(8,128)S(1)} %fusion.67, f32[32,128,128]{2,0,1:T(8,128)S(1)} %fusion.69), kind=kOutput, calls=%fused_computation.12.clone.1 | convolution fusion | flops 805306368 | bytes 6291456 | tf_op jit(solution)/shard_map/while/body/eval_jaxpr/ptu,puv->ptv/dot_general | solution.py:90
  210.3 2.8 fusion.71
  213.0 53.5 %all_to_all.5 = f32[8,8,128,128]{3,1,2,0:T(8,128)} all-to-all(f32[8,8,128,128]{3,1,2,0:T(8,128)} %get-tuple-element.52), channel_id=1, replica_groups=mesh['rows'=8,'blk'=4] {'rows'}, dimensions={0} | all-to-all | bytes 8388608 | tf_op jit(solution)/shard_map/all_to_all | solution.py:97
  266.6 2.5 reduce_sum.59
  269.1 1.5 fusion.33
  (70 shorter events, 0.4 us)
Async XLA Ops:
  6.5 1.1 copy-start
  6.5 4.6 %copy-start.3 = (s32[8,32]{1,0:T(8,128)S(1)}, s32[8,32]{1,0:T(8,128)}, u32[]{:S(2)}) copy-start(s32[8,32]{1,0:T(8,128)} %param.15) | copy-start | bytes 3076
  6.5 4.7 %copy-start.6 = (s32[8]{0:T(128)S(1)}, s32[8]{0:T(128)}, u32[]{:S(2)}) copy-start(s32[8]{0:T(128)} %param.17) | copy-start | bytes 100
  6.5 4.9 %copy-start.4 = (s32[8,32]{1,0:T(8,128)S(1)}, s32[8,32]{1,0:T(8,128)}, u32[]{:S(2)}) copy-start(s32[8,32]{1,0:T(8,128)} %param.16) | copy-start | bytes 3076
  6.5 5.0 %copy-start.5 = (s32[8,32]{1,0:T(8,128)S(1)}, s32[8,32]{1,0:T(8,128)}, u32[]{:S(2)}) copy-start(s32[8,32]{1,0:T(8,128)} %param.14) | copy-start | bytes 3076
  6.5 70.9 %all-gather.2.cloned.1.call-start = ((), (), s32[]{:S(2)}) async-start(), calls=%async_computation.1 | async-start | bytes 3932160 | tf_op jit(solution)/shard_map/all_gather | solution.py:83
  12.4 5.0 %collective-permute-start = (s32[4,1,32]{2,0,1:T(4,128)S(1)}, s32[4,1,32]{2,0,1:T(4,128)S(1)}, u32[]{:S(2)}, u32[]{:S(2)}) collective-permute-start(s32[4,1,32]{2,0,1:T(4,128)S(1)} %get-tuple-element.103), channel_id=1, source_target_pairs={{0,4},{4,0},{8,12},{12,8},{16,20},{20,16},{24,28},{28,24},{1,5},{5... | collective-permute-start | bytes 1544 | tf_op jit(solution)/shard_map/ppermute | solution.py:76
  13.0 7.1 %collective-permute-start.1 = (s32[4,1,32]{2,0,1:T(4,128)S(1)}, s32[4,1,32]{2,0,1:T(4,128)S(1)}, u32[]{:S(2)}, u32[]{:S(2)}) collective-permute-start(s32[4,1,32]{2,0,1:T(4,128)S(1)} %get-tuple-element.102), channel_id=1, source_target_pairs={{0,8},{4,12},{8,0},{12,4},{16,24},{20,28},{24,16},{28,20},{1,9},{5... | collective-permute-start | bytes 1544 | tf_op jit(solution)/shard_map/ppermute | solution.py:76
  15.5 4.7 %collective-permute-start.2 = (s32[4,1,32]{2,0,1:T(4,128)S(1)}, s32[4,1,32]{2,0,1:T(4,128)S(1)}, u32[]{:S(2)}, u32[]{:S(2)}) collective-permute-start(s32[4,1,32]{2,0,1:T(4,128)S(1)} %get-tuple-element.101), channel_id=1, source_target_pairs={{0,12},{4,8},{8,4},{12,0},{16,28},{20,24},{24,20},{28,16},{1,13},{... | collective-permute-start | bytes 1544 | tf_op jit(solution)/shard_map/ppermute | solution.py:76
  15.6 4.7 %collective-permute-start.3 = (s32[4,1,32]{2,0,1:T(4,128)S(1)}, s32[4,1,32]{2,0,1:T(4,128)S(1)}, u32[]{:S(2)}, u32[]{:S(2)}) collective-permute-start(s32[4,1,32]{2,0,1:T(4,128)S(1)} %get-tuple-element.100), channel_id=1, source_target_pairs={{0,16},{4,20},{8,24},{12,28},{16,0},{20,4},{24,8},{28,12},{1,17},{... | collective-permute-start | bytes 1544 | tf_op jit(solution)/shard_map/ppermute | solution.py:76
  17.3 3.0 %collective-permute-start.4 = (s32[4,1,32]{2,0,1:T(4,128)S(1)}, s32[4,1,32]{2,0,1:T(4,128)S(1)}, u32[]{:S(2)}, u32[]{:S(2)}) collective-permute-start(s32[4,1,32]{2,0,1:T(4,128)S(1)} %get-tuple-element.99), channel_id=1, source_target_pairs={{0,20},{4,16},{8,28},{12,24},{16,4},{20,0},{24,12},{28,8},{1,21},{... | collective-permute-start | bytes 1544 | tf_op jit(solution)/shard_map/ppermute | solution.py:76
  17.4 4.5 %collective-permute-start.5 = (s32[4,1,32]{2,0,1:T(4,128)S(1)}, s32[4,1,32]{2,0,1:T(4,128)S(1)}, u32[]{:S(2)}, u32[]{:S(2)}) collective-permute-start(s32[4,1,32]{2,0,1:T(4,128)S(1)} %get-tuple-element.98), channel_id=1, source_target_pairs={{0,24},{4,28},{8,16},{12,20},{16,8},{20,12},{24,0},{28,4},{1,25},{... | collective-permute-start | bytes 1544 | tf_op jit(solution)/shard_map/ppermute | solution.py:76
  20.1 3.9 %collective-permute-start.6 = (s32[4,1,32]{2,0,1:T(4,128)S(1)}, s32[4,1,32]{2,0,1:T(4,128)S(1)}, u32[]{:S(2)}, u32[]{:S(2)}) collective-permute-start(s32[4,1,32]{2,0,1:T(4,128)S(1)} %get-tuple-element.97), channel_id=1, source_target_pairs={{0,28},{4,24},{8,20},{12,16},{16,12},{20,8},{24,4},{28,0},{1,29},{... | collective-permute-start | bytes 1544 | tf_op jit(solution)/shard_map/ppermute | solution.py:76
  77.5 6.2 %copy-start.1 = (f32[48,128,128]{2,1,0:T(8,128)S(1)}, f32[48,128,128]{2,1,0:T(8,128)}, u32[]{:S(2)}) copy-start(f32[48,128,128]{2,1,0:T(8,128)} %get-tuple-element.184) | copy-start | bytes 9437188 | tf_op jit(solution)/shard_map/while
  94.4 6.2 %copy-start.1 = (f32[48,128,128]{2,1,0:T(8,128)S(1)}, f32[48,128,128]{2,1,0:T(8,128)}, u32[]{:S(2)}) copy-start(f32[48,128,128]{2,1,0:T(8,128)} %get-tuple-element.184) | copy-start | bytes 9437188 | tf_op jit(solution)/shard_map/while
  111.4 6.2 %copy-start.1 = (f32[48,128,128]{2,1,0:T(8,128)S(1)}, f32[48,128,128]{2,1,0:T(8,128)}, u32[]{:S(2)}) copy-start(f32[48,128,128]{2,1,0:T(8,128)} %get-tuple-element.184) | copy-start | bytes 9437188 | tf_op jit(solution)/shard_map/while
  128.3 6.2 %copy-start.1 = (f32[48,128,128]{2,1,0:T(8,128)S(1)}, f32[48,128,128]{2,1,0:T(8,128)}, u32[]{:S(2)}) copy-start(f32[48,128,128]{2,1,0:T(8,128)} %get-tuple-element.184) | copy-start | bytes 9437188 | tf_op jit(solution)/shard_map/while
  145.3 6.2 %copy-start.1 = (f32[48,128,128]{2,1,0:T(8,128)S(1)}, f32[48,128,128]{2,1,0:T(8,128)}, u32[]{:S(2)}) copy-start(f32[48,128,128]{2,1,0:T(8,128)} %get-tuple-element.184) | copy-start | bytes 9437188 | tf_op jit(solution)/shard_map/while
  162.2 6.2 %copy-start.1 = (f32[48,128,128]{2,1,0:T(8,128)S(1)}, f32[48,128,128]{2,1,0:T(8,128)}, u32[]{:S(2)}) copy-start(f32[48,128,128]{2,1,0:T(8,128)} %get-tuple-element.184) | copy-start | bytes 9437188 | tf_op jit(solution)/shard_map/while
  179.2 6.2 %copy-start.1 = (f32[48,128,128]{2,1,0:T(8,128)S(1)}, f32[48,128,128]{2,1,0:T(8,128)}, u32[]{:S(2)}) copy-start(f32[48,128,128]{2,1,0:T(8,128)} %get-tuple-element.184) | copy-start | bytes 9437188 | tf_op jit(solution)/shard_map/while
  196.1 6.2 %copy-start.1 = (f32[48,128,128]{2,1,0:T(8,128)S(1)}, f32[48,128,128]{2,1,0:T(8,128)}, u32[]{:S(2)}) copy-start(f32[48,128,128]{2,1,0:T(8,128)} %get-tuple-element.184) | copy-start | bytes 9437188 | tf_op jit(solution)/shard_map/while
  266.6 2.5 copy-start.2
Sparse Core Ops, SparseCore 0:
  11.3 66.1 all-gather.1
